TPU v7x, 128 devices: a whole 4x4x4 slice. The times are simulated.
128 devices in a mesh: pix: 8 (over y_hi, x), mode: 16 (over z, y_lo, core).
Axes of the slice: x: 4, y: 4 (y_hi: 2, y_lo: 2; y = y_hi * 2 + y_lo), z: 4, core: 2. Of those that a mesh axis runs over, the one named last changes fastest.
Arguments:
- matrix: float32 [2, 4096, 32768], P(None, 'pix', 'mode'), may hold values from -0.03125 to 0.03125
- calibration_fields: float32 [2, 4096, 512], P(None, 'pix', 'mode'), may hold values from -0.25 to 0.25
- patterns: int32 [32768, 512], P('mode'), may hold values from 0 to 255
- targets: int32 [4096, 128], P('pix'), may hold values from 0 to 255
- phases: float32 [32768, 128], P('mode'), may hold values from -3.140625 to 3.140625
Outputs:
- updated: float32 [2, 4096, 32768], P(None, 'pix', 'mode')
- slm_field: float32 [2, 32768, 128], P(None, 'mode')
- camera_field: float32 [2, 4096, 128], P(None, 'pix')
All inputs are finite; a program needn't handle non-finite values.
Results may differ from a plain program's by a relative error of at most 0.00014.
Values sent between devices are 32-bit elements; how exact they have to be, the bound alone decides.
No kernel may reach another device: no remote copies, remote signals or barrier semaphores. Data moves between devices by JAX's collectives and lax.ppermute only.
A program may use at most 128 MiB of HBM per device.

v0:
```python
import math
import jax
import jax.numpy as jnp
from jax import lax
from jax.sharding import PartitionSpec as P

LEVELS = 256
ITERS = 2


def matmul(left, right):
    return jnp.dot(left, right, precision=lax.Precision.HIGHEST, preferred_element_type=jnp.float32)


def matmul_nt(left, right):
    return lax.dot_general(
        left,
        right,
        (((1,), (1,)), ((), ())),
        precision=lax.Precision.HIGHEST,
        preferred_element_type=jnp.float32,
    )


def matmul_tn(left, right):
    return lax.dot_general(
        left,
        right,
        (((0,), (0,)), ((), ())),
        precision=lax.Precision.HIGHEST,
        preferred_element_type=jnp.float32,
    )


def camera_rows(real_new, imag_new, slm_now, width):
    real_times = matmul(real_new, slm_now)
    imag_times = matmul(imag_new, slm_now)
    return jnp.concatenate(
        [
            real_times[:, :width] - imag_times[:, width:],
            real_times[:, width:] + imag_times[:, :width],
        ],
        axis=1,
    )


def slm_rows(real_new, imag_new, shaped, width):
    real_times = matmul_tn(real_new, shaped)
    imag_times = matmul_tn(imag_new, shaped)
    return jnp.concatenate(
        [
            real_times[:, :width] + imag_times[:, width:],
            real_times[:, width:] - imag_times[:, :width],
        ],
        axis=1,
    )


def clamp_scale(source, floor_value, width):
    magnitude = jnp.sqrt(
        source[:, :width] * source[:, :width] + source[:, width:] * source[:, width:]
    )
    return 1.0 / jnp.maximum(magnitude, floor_value)


def project(camera, amplitude, width):
    factor = amplitude * clamp_scale(camera, 0.5, width)
    return camera * jnp.concatenate([factor, factor], axis=1)


def normalize(back_field, floor_value, width):
    factor = clamp_scale(back_field, floor_value, width)
    return back_field * jnp.concatenate([factor, factor], axis=1)


def camera_pass(real_new, imag_new, slm_now, amplitude, width, shaping):
    camera = lax.psum(camera_rows(real_new, imag_new, slm_now, width), "mode")
    if shaping:
        camera = project(camera, amplitude, width)
    return camera


def slm_pass(real_new, imag_new, shaped, floor_value, width):
    back_field = lax.psum(slm_rows(real_new, imag_new, shaped, width), "pix")
    slm_now = normalize(back_field, floor_value, width)
    return slm_now


def body(matrix, calibration_fields, patterns, targets, phases):
    real_start = matrix[0]
    imag_start = matrix[1]
    pix_rows, mode_cols = real_start.shape
    pix_total = pix_rows * lax.axis_size("pix")
    mode_total = mode_cols * lax.axis_size("mode")
    width = targets.shape[1]
    angles = patterns.astype(jnp.float32) * (2.0 * math.pi / LEVELS)
    cosine = jnp.cos(angles) / math.sqrt(mode_total)
    sine_table = jnp.sin(angles) / math.sqrt(mode_total)
    panel_whole = lax.all_gather(calibration_fields, "mode", axis=2, tiled=True)
    real_new = real_start + (
        matmul_nt(panel_whole[0], cosine) + matmul_nt(panel_whole[1], sine_table)
    )
    imag_new = imag_start + (
        matmul_nt(panel_whole[1], cosine) - matmul_nt(panel_whole[0], sine_table)
    )
    amplitude = targets.astype(jnp.float32) / 128.0
    floor_value = 0.5 * math.sqrt(pix_total / mode_total)
    slm_now = jnp.concatenate([jnp.cos(phases), jnp.sin(phases)], axis=1)
    for repeat in range(ITERS):
        shaped = camera_pass(real_new, imag_new, slm_now, amplitude, width, True)
        slm_now = slm_pass(real_new, imag_new, shaped, floor_value, width)
    camera = camera_pass(real_new, imag_new, slm_now, amplitude, width, False)
    updated = jnp.stack([real_new, imag_new])
    slm_field = jnp.stack([slm_now[:, :width], slm_now[:, width:]])
    camera_field = jnp.stack([camera[:, :width], camera[:, width:]])
    return (updated, slm_field, camera_field)


def solution(mesh):
    in_specs = (
        P(None, "pix", "mode"),
        P(None, "pix", "mode"),
        P("mode", None),
        P("pix", None),
        P("mode", None),
    )
    out_specs = (P(None, "pix", "mode"), P(None, "mode", None), P(None, "pix", None))
    return jax.shard_map(body, mesh=mesh, in_specs=in_specs, out_specs=out_specs, check_vma=False)
```

profile of v0, /device:TPU:1, one launch (start us, length us, event | category | flops | bytes accessed | tf_op | source)
XLA Modules:
  0.0 747.0 jit_solution(13222708839434813150)
XLA Ops:
  7.9 7.9 %fusion.54 = (f32[1,512,2048]{2,1,0:T(8,128)}, f32[1,512,2048]{2,1,0:T(8,128)}) fusion(f32[2,512,2048]{2,1,0:T(8,128)} %param.5), kind=kLoop, calls=%fused_computation.97 | loop fusion | bytes 16777216 | tf_op jit(solution)/shard_map/slice | solution.py:90
  15.8 5.5 copy.14
  21.3 5.5 copy.15
  26.8 3.7 fusion.55
  30.5 16.7 %all-gather.2.cloned.1.call-done = f32[2,512,512]{1,2,0:T(8,128)} async-done(((f32[2,512,32]{1,2,0:T(8,128)}), f32[2,512,512]{1,2,0:T(8,128)}) %all-gather.2.cloned.1.call-update) | async-done | bytes 2097168 | tf_op jit(solution)/shard_map/all_gather | solution.py:99
  47.2 22.6 %fusion.1 = f32[2048,512]{1,0:T(8,128)S(1)} fusion(s32[2048,512]{1,0:T(8,128)} %param.7, f32[2,512,512]{1,2,0:T(8,128)} %all-gather.2.cloned.1.call-done), kind=kOutput, calls=%fused_computation.7 | convolution fusion | flops 6445596672 | bytes 9437184 | tf_op jit(solution)/shard_map/dot_general | solution.py:16
  69.8 21.4 %bitcast_add_fusion.1 = f32[512,2048]{0,1:T(8,128)S(1)} fusion(f32[1,512,2048]{1,2,0:T(8,128)S(1)} %copy-done.9, f32[2048,512]{1,0:T(8,128)S(1)} %fusion.1, s32[2048,512]{1,0:T(8,128)S(1)} %copy-done.7, f32[2,512,512]{1,2,0:T(8,128)S(1)} %copy-done.11), kind=kOutput, calls=%fused_computation.2 | convolution fusion | flops 6447693824 | bytes 17825792 | tf_op jit(solution)/shard_map/dot_general | solution.py:16
  91.2 4.3 fusion.13
  95.6 20.7 %fusion = f32[2048,512]{1,0:T(8,128)S(1)} fusion(s32[2048,512]{1,0:T(8,128)S(1)} %copy-done.7, f32[2,512,512]{1,2,0:T(8,128)S(1)} %copy-done.11), kind=kOutput, calls=%fused_computation.6 | convolution fusion | flops 6445596672 | bytes 9437184 | tf_op jit(solution)/shard_map/dot_general | solution.py:16
  116.3 21.8 %bitcast_add_fusion = f32[512,2048]{0,1:T(8,128)S(1)} fusion(f32[1,512,2048]{1,2,0:T(8,128)S(1)} %copy-done.8, f32[2048,512]{1,0:T(8,128)S(1)} %fusion, s32[2048,512]{1,0:T(8,128)S(1)} %copy-done.7, f32[2,512,512]{1,2,0:T(8,128)S(1)} %copy-done.11), kind=kOutput, calls=%fused_computation.1 | convolution fusion | flops 6447693824 | bytes 17825792 | tf_op jit(solution)/shard_map/dot_general | solution.py:16
  138.1 3.9 fusion.12
  143.2 118.4 %all-reduce.6.cloned.1.call-done = f32[512,256]{0,1:T(8,128)} async-done(((f32[512,256]{0,1:T(8,128)}), f32[512,256]{0,1:T(8,128)}) %all-reduce.6.cloned.1.call-update) | async-done | bytes 524304 | tf_op jit(solution)/shard_map/psum | solution.py:77
  263.0 6.5 fusion.27
  269.4 3.9 fusion.26
  273.7 1.5 pad_maximum_fusion.2
  275.2 88.9 %all-reduce.8.cloned.1.call-done = f32[2048,256]{0,1:T(8,128)} async-done(((f32[2048,256]{0,1:T(8,128)}), f32[2048,256]{0,1:T(8,128)}) %all-reduce.8.cloned.1.call-update) | async-done | bytes 2097168 | tf_op jit(solution)/shard_map/psum | solution.py:84
  364.1 2.1 fusion.23
  366.3 6.1 fusion.15
  372.5 4.0 fusion.14
  377.4 122.4 %all-reduce.10.cloned.1.call-done = f32[512,256]{0,1:T(8,128)} async-done(((f32[512,256]{0,1:T(8,128)}), f32[512,256]{0,1:T(8,128)}) %all-reduce.10.cloned.1.call-update) | async-done | bytes 524304 | tf_op jit(solution)/shard_map/psum | solution.py:77
  501.2 6.5 fusion.25
  507.7 3.9 fusion.24
  512.0 1.5 pad_maximum_fusion.3
  513.5 7.7 %pad_maximum_fusion = f32[2,512,2048]{1,2,0:T(8,128)} fusion(f32[1,512,2048]{1,2,0:T(8,128)} %bitcast.39, f32[1,512,2048]{1,2,0:T(8,128)} %bitcast.38), kind=kLoop, calls=%fused_computation | loop fusion | flops 2097152 | bytes 16777216 | tf_op jit(solution)/shard_map/stack | solution.py:113
  521.3 8.9 %copy.11 = f32[2,512,2048]{2,1,0:T(8,128)} copy(f32[2,512,2048]{1,2,0:T(8,128)} %pad_maximum_fusion) | data formatting | bytes 16777216
  530.2 72.3 %all-reduce.12.cloned.1.call-done = f32[2048,256]{0,1:T(8,128)} async-done(((f32[2048,256]{0,1:T(8,128)}), f32[2048,256]{0,1:T(8,128)}) %all-reduce.12.cloned.1.call-update) | async-done | bytes 2097168 | tf_op jit(solution)/shard_map/psum | solution.py:84
  602.5 2.1 fusion.19
  604.6 1.8 maximum_multiply_fusion.1
  606.4 3.8 fusion.56
  610.3 3.8 fusion.57
  615.5 1.8 copy.12
  617.3 120.2 %all-reduce.14.cloned.1.call-done = f32[512,256]{0,1:T(8,128)} async-done(((f32[512,256]{0,1:T(8,128)}), f32[512,256]{0,1:T(8,128)}) %all-reduce.14.cloned.1.call-update) | async-done | bytes 524304 | tf_op jit(solution)/shard_map/psum | solution.py:77
  (60 shorter events, 9.9 us)
Async XLA Ops:
  7.2 40.0 %all-gather.2.cloned.1.call-start = ((), (), s32[]{:S(2)}) async-start(), calls=%async_computation | async-start | bytes 2228224 | tf_op jit(solution)/shard_map/all_gather | solution.py:99
  7.9 253.7 %all-reduce.6.cloned.1.call-start = ((), (), s32[]{:S(2)}) async-start(), calls=%async_computation.1 | async-start | bytes 1048576 | tf_op jit(solution)/shard_map/psum | solution.py:77
  21.3 5.5 copy-start.14
  47.2 22.6 %copy-start.7 = (s32[2048,512]{1,0:T(8,128)S(1)}, s32[2048,512]{1,0:T(8,128)}, u32[]{:S(2)}) copy-start(s32[2048,512]{1,0:T(8,128)} %param.7) | copy-start | bytes 12582916
  47.2 22.6 %copy-start.9 = (f32[1,512,2048]{1,2,0:T(8,128)S(1)}, f32[1,512,2048]{1,2,0:T(8,128)}, u32[]{:S(2)}) copy-start(f32[1,512,2048]{1,2,0:T(8,128)} %copy.14) | copy-start | bytes 12582916
  47.2 22.6 %copy-start.11 = (f32[2,512,512]{1,2,0:T(8,128)S(1)}, f32[2,512,512]{1,2,0:T(8,128)}, u32[]{:S(2)}) copy-start(f32[2,512,512]{1,2,0:T(8,128)} %all-gather.2.cloned.1.call-done) | copy-start | bytes 6291460
  91.2 4.4 copy-start
  95.6 20.7 %copy-start.8 = (f32[1,512,2048]{1,2,0:T(8,128)S(1)}, f32[1,512,2048]{1,2,0:T(8,128)}, u32[]{:S(2)}) copy-start(f32[1,512,2048]{1,2,0:T(8,128)} %copy.15) | copy-start | bytes 12582916
  138.1 3.9 copy-start.2
  138.1 4.9 copy-start.15
  143.0 221.1 %all-reduce.8.cloned.1.call-start = ((), (), s32[]{:S(2)}) async-start(), calls=%async_computation.2 | async-start | bytes 4194304 | tf_op jit(solution)/shard_map/psum | solution.py:84
  261.6 7.8 %copy-start.3 = (f32[512,2048]{0,1:T(8,128)S(1)}, f32[512,2048]{0,1:T(8,128)}, u32[]{:S(2)}) copy-start(f32[512,2048]{0,1:T(8,128)} %copy-done.2) | copy-start | bytes 12582916
  261.6 7.8 %copy-start.12 = (f32[512,256]{0,1:T(8,128)S(1)}, f32[512,256]{0,1:T(8,128)}, u32[]{:S(2)}) copy-start(f32[512,256]{0,1:T(8,128)} %all-reduce.6.cloned.1.call-done) | copy-start | bytes 1572868
  275.2 224.7 %all-reduce.10.cloned.1.call-start = ((), (), s32[]{:S(2)}) async-start(), calls=%async_computation.3 | async-start | bytes 1048576 | tf_op jit(solution)/shard_map/psum | solution.py:77
  364.1 2.2 copy-start.10
  366.3 6.2 copy-start.4
  377.4 225.1 %all-reduce.12.cloned.1.call-start = ((), (), s32[]{:S(2)}) async-start(), calls=%async_computation.4 | async-start | bytes 4194304 | tf_op jit(solution)/shard_map/psum | solution.py:84
  499.8 7.9 %copy-start.5 = (f32[512,2048]{0,1:T(8,128)S(1)}, f32[512,2048]{0,1:T(8,128)}, u32[]{:S(2)}) copy-start(f32[512,2048]{0,1:T(8,128)} %copy-done.2) | copy-start | bytes 12582916
  499.8 7.9 %copy-start.13 = (f32[512,256]{0,1:T(8,128)S(1)}, f32[512,256]{0,1:T(8,128)}, u32[]{:S(2)}) copy-start(f32[512,256]{0,1:T(8,128)} %all-reduce.10.cloned.1.call-done) | copy-start | bytes 1572868
  513.5 224.1 %all-reduce.14.cloned.1.call-start = ((), (), s32[]{:S(2)}) async-start(), calls=%async_computation.5 | async-start | bytes 1048576 | tf_op jit(solution)/shard_map/psum | solution.py:77
  602.5 3.9 copy-start.1
  606.4 3.9 copy-start.6
Sparse Core Ops, SparseCore 0:
  9.6 37.4 all-gather.1
  143.1 118.4 all-reduce.5
  275.3 88.7 all-reduce.7
  377.5 122.3 all-reduce.9
  513.6 88.8 all-reduce.11
  615.2 122.3 all-reduce.13
where the time goes:
time: 756 us; the launch traced here: 747 us
  waiting for transfers between devices  540 us (71%)
  matrix products  133 us (18%)
  local copies, waits for them, and re-layouts  35.9 us (5%)
  other arithmetic  23 us (3%)
  between operations  15 us (2%)
    psum x3, waiting for transfers between devices, camera_pass(): camera = lax.psum(camera_rows(real_new, imag_new, slm_now, width), 'mode')  361 us
    psum x2, waiting for transfers between devices, slm_pass(): back_field = lax.psum(slm_rows(real_new, imag_new, shaped, width), 'pix')  161 us
    dot_general x4, matrix products, matmul_nt(): lax.dot_general(left, right, (((1,), (1,)), ((), ())), precision=lax.Prec...  86.5 us
    dot_general x6, matrix products, matmul(): jnp.dot(left, right, precision=lax.Precision.HIGHEST, preferred_element_t...  26 us
    unnamed x38, local copies, waits for them, and re-layouts  23 us
    dot_general x4, matrix products, matmul_tn(): lax.dot_general(left, right, (((0,), (0,)), ((), ())), precision=lax.Prec...  20.8 us
    all_gather x1, waiting for transfers between devices, body(): panel_whole = lax.all_gather(calibration_fields, 'mode', axis=2, tiled=True)  16.7 us
  transfers between devices with their start and end apart: 6, of which 6 were waited for; matrix products, arithmetic and copies ran while one was open for 6% of the time, Pallas kernels for 0%

commit v1 on v0

--- a/solution.py
+++ b/solution.py
@@ -6,6 +6,11 @@
 
 LEVELS = 256
 ITERS = 2
+
+
+def summed_here(x, mesh_axis):
+    terms = lax.all_gather(x, mesh_axis)
+    return jnp.sum(terms, axis=0)
 
 
 def matmul(left, right):
@@ -81,7 +86,7 @@
 
 
 def slm_pass(real_new, imag_new, shaped, floor_value, width):
-    back_field = lax.psum(slm_rows(real_new, imag_new, shaped, width), "pix")
+    back_field = summed_here(slm_rows(real_new, imag_new, shaped, width), "pix")
     slm_now = normalize(back_field, floor_value, width)
     return slm_now
 

time: 756 us -> 980 us (1.30)
  waiting for transfers between devices: 540 us -> 723 us
  local copies, waits for them, and re-layouts: 35.9 us -> 72.8 us
    all_gather x0 -> x2, waiting for transfers between devices: none -> 354 us  [summed_here(): terms = lax.all_gather(x, mesh_axis)]
    psum x2 -> x0, waiting for transfers between devices: 161 us -> none  [slm_pass(): back_field = lax.psum(slm_rows(real_new, imag_new, shaped, width), 'pix')]
    unnamed x38 -> x40, local copies, waits for them, and re-layouts: 23 us -> 60 us
    reduce_sum x0 -> x2, other arithmetic: none -> 11.2 us  [summed_here(): return jnp.sum(terms, axis=0)]
  transfers between devices with their start and end apart: 6 -> 6, of which waited for: 6 -> 6; matrix products, arithmetic and copies ran while one was open for 6% -> 4% of each run, Pallas kernels for 0% -> 0%
where the time goes in v1:
time: 980 us; the launch traced here: 971 us
  waiting for transfers between devices  723 us (74%)
  matrix products  131 us (13%)
  local copies, waits for them, and re-layouts  72.8 us (7%)
  other arithmetic  29.2 us (3%)
  between operations  15 us (2%)
    all_gather x2, waiting for transfers between devices, summed_here(): terms = lax.all_gather(x, mesh_axis)  354 us
    psum x3, waiting for transfers between devices, camera_pass(): camera = lax.psum(camera_rows(real_new, imag_new, slm_now, width), 'mode')  351 us
    dot_general x4, matrix products, matmul_nt(): lax.dot_general(left, right, (((1,), (1,)), ((), ())), precision=lax.Prec...  86.6 us
    unnamed x40, local copies, waits for them, and re-layouts  60 us
    dot_general x6, matrix products, matmul(): jnp.dot(left, right, precision=lax.Precision.HIGHEST, preferred_element_t...  23.7 us
    dot_general x4, matrix products, matmul_tn(): lax.dot_general(left, right, (((0,), (0,)), ((), ())), precision=lax.Prec...  20.9 us
  transfers between devices with their start and end apart: 6, of which 6 were waited for; matrix products, arithmetic and copies ran while one was open for 4% of the time, Pallas kernels for 0%

profile of v1, /device:TPU:1, one launch (start us, length us, event | category | flops | bytes accessed | tf_op | source)
XLA Modules:
  0.0 971.3 jit_solution(8058897451236706472)
XLA Ops:
  7.9 7.9 fusion.54
  15.8 5.5 copy.19
  21.3 5.5 copy.20
  26.8 3.7 fusion.55
  30.5 16.7 %all-gather.6.cloned.1.call-done = f32[2,512,512]{1,2,0:T(8,128)} async-done(((f32[2,512,32]{1,2,0:T(8,128)}), f32[2,512,512]{1,2,0:T(8,128)}) %all-gather.6.cloned.1.call-update) | async-done | bytes 2097168 | tf_op jit(solution)/shard_map/all_gather | solution.py:104
  47.2 22.8 %fusion.1 = f32[2048,512]{1,0:T(8,128)S(1)} fusion(s32[2048,512]{1,0:T(8,128)} %param.7, f32[2,512,512]{1,2,0:T(8,128)} %all-gather.6.cloned.1.call-done), kind=kOutput, calls=%fused_computation.9 | convolution fusion | flops 6445596672 | bytes 9437184 | tf_op jit(solution)/shard_map/dot_general | solution.py:21
  70.0 21.4 %bitcast_add_fusion.1 = f32[512,2048]{0,1:T(8,128)S(1)} fusion(f32[1,512,2048]{1,2,0:T(8,128)S(1)} %copy-done.10, f32[2048,512]{1,0:T(8,128)S(1)} %fusion.1, s32[2048,512]{1,0:T(8,128)S(1)} %copy-done.8, f32[2,512,512]{1,2,0:T(8,128)S(1)} %copy-done.11), kind=kOutput, calls=%fused_computation.4 | convolution fusion | flops 6447693824 | bytes 17825792 | tf_op jit(solution)/shard_map/dot_general | solution.py:21
  91.4 4.2 fusion.13
  95.5 21.0 %fusion = f32[2048,512]{1,0:T(8,128)S(1)} fusion(s32[2048,512]{1,0:T(8,128)S(1)} %copy-done.8, f32[2,512,512]{1,2,0:T(8,128)S(1)} %copy-done.11), kind=kOutput, calls=%fused_computation.8 | convolution fusion | flops 6445596672 | bytes 9437184 | tf_op jit(solution)/shard_map/dot_general | solution.py:21
  116.5 21.6 %bitcast_add_fusion = f32[512,2048]{0,1:T(8,128)S(1)} fusion(f32[1,512,2048]{1,2,0:T(8,128)S(1)} %copy-done.9, f32[2048,512]{1,0:T(8,128)S(1)} %fusion, s32[2048,512]{1,0:T(8,128)S(1)} %copy-done.8, f32[2,512,512]{1,2,0:T(8,128)S(1)} %copy-done.11), kind=kOutput, calls=%fused_computation.3 | convolution fusion | flops 6447693824 | bytes 17825792 | tf_op jit(solution)/shard_map/dot_general | solution.py:21
  138.1 3.9 fusion.12
  143.2 118.4 %all-reduce.4.cloned.1.call-done = f32[512,256]{0,1:T(8,128)} async-done(((f32[512,256]{0,1:T(8,128)}), f32[512,256]{0,1:T(8,128)}) %all-reduce.4.cloned.1.call-update) | async-done | bytes 524304 | tf_op jit(solution)/shard_map/psum | solution.py:82
  262.9 6.6 fusion.26
  269.6 3.9 fusion.27
  275.4 185.5 %all-gather.8.cloned.1.call-done = f32[16384,256]{0,1:T(8,128)} async-done(((f32[2048,256]{0,1:T(8,128)}), f32[16384,256]{0,1:T(8,128)}) %all-gather.8.cloned.1.call-update) | async-done | bytes 16777232 | tf_op jit(solution)/shard_map/all_gather | solution.py:12
  460.9 17.6 %copy.21 = f32[32,8,8,2048]{3,2,1,0:T(8,128)S(1)} copy(f32[32,8,8,2048]{3,1,2,0:T(8,128)} %bitcast.51) | data formatting | bytes 33554432
  478.5 5.6 bitcast_reduce_fusion.1
  484.5 4.0 fusion.14
  488.4 4.0 fusion.15
  493.4 117.6 %all-reduce.6.cloned.1.call-done = f32[512,256]{0,1:T(8,128)} async-done(((f32[512,256]{0,1:T(8,128)}), f32[512,256]{0,1:T(8,128)}) %all-reduce.6.cloned.1.call-update) | async-done | bytes 524304 | tf_op jit(solution)/shard_map/psum | solution.py:82
  612.3 6.4 fusion.24
  618.8 3.9 fusion.25
  624.6 7.7 pad_maximum_fusion
  632.3 9.4 copy.16
  641.7 168.4 %all-gather.10.cloned.1.call-done = f32[16384,256]{0,1:T(8,128)} async-done(((f32[2048,256]{0,1:T(8,128)}), f32[16384,256]{0,1:T(8,128)}) %all-gather.10.cloned.1.call-update) | async-done | bytes 16777232 | tf_op jit(solution)/shard_map/all_gather | solution.py:12
  810.1 17.6 %copy.22 = f32[32,8,8,2048]{3,2,1,0:T(8,128)S(1)} copy(f32[32,8,8,2048]{3,1,2,0:T(8,128)} %bitcast.50) | data formatting | bytes 33554432
  827.7 5.7 bitcast_reduce_fusion
  834.0 1.5 copy-done.4
  835.6 3.8 fusion.56
  839.4 3.8 fusion.57
  844.7 1.8 copy.17
  846.5 115.4 %all-reduce.8.cloned.1.call-done = f32[512,256]{0,1:T(8,128)} async-done(((f32[512,256]{0,1:T(8,128)}), f32[512,256]{0,1:T(8,128)}) %all-reduce.8.cloned.1.call-update) | async-done | bytes 524304 | tf_op jit(solution)/shard_map/psum | solution.py:82
  (64 shorter events, 13.7 us)
Async XLA Ops:
  7.2 40.0 %all-gather.6.cloned.1.call-start = ((), (), s32[]{:S(2)}) async-start(), calls=%async_computation | async-start | bytes 2228224 | tf_op jit(solution)/shard_map/all_gather | solution.py:104
  7.9 253.7 %all-reduce.4.cloned.1.call-start = ((), (), s32[]{:S(2)}) async-start(), calls=%async_computation.1 | async-start | bytes 1048576 | tf_op jit(solution)/shard_map/psum | solution.py:82
  21.3 5.5 copy-start.14
  47.2 22.8 %copy-start.8 = (s32[2048,512]{1,0:T(8,128)S(1)}, s32[2048,512]{1,0:T(8,128)}, u32[]{:S(2)}) copy-start(s32[2048,512]{1,0:T(8,128)} %param.7) | copy-start | bytes 12582916
  47.2 22.8 %copy-start.10 = (f32[1,512,2048]{1,2,0:T(8,128)S(1)}, f32[1,512,2048]{1,2,0:T(8,128)}, u32[]{:S(2)}) copy-start(f32[1,512,2048]{1,2,0:T(8,128)} %copy.19) | copy-start | bytes 12582916
  47.2 22.8 %copy-start.11 = (f32[2,512,512]{1,2,0:T(8,128)S(1)}, f32[2,512,512]{1,2,0:T(8,128)}, u32[]{:S(2)}) copy-start(f32[2,512,512]{1,2,0:T(8,128)} %all-gather.6.cloned.1.call-done) | copy-start | bytes 6291460
  91.3 4.2 copy-start
  95.5 21.0 %copy-start.9 = (f32[1,512,2048]{1,2,0:T(8,128)S(1)}, f32[1,512,2048]{1,2,0:T(8,128)}, u32[]{:S(2)}) copy-start(f32[1,512,2048]{1,2,0:T(8,128)} %copy.20) | copy-start | bytes 12582916
  138.1 3.9 copy-start.5
  138.1 4.9 copy-start.15
  143.0 317.9 %all-gather.8.cloned.1.call-start = ((), (), s32[]{:S(2)}) async-start(), calls=%async_computation.4 | async-start | bytes 18874368 | tf_op jit(solution)/shard_map/all_gather | solution.py:12
  261.6 8.0 copy-start.1
  261.6 8.0 copy-start.12
  275.3 335.7 %all-reduce.6.cloned.1.call-start = ((), (), s32[]{:S(2)}) async-start(), calls=%async_computation.2 | async-start | bytes 1048576 | tf_op jit(solution)/shard_map/psum | solution.py:82
  478.5 6.0 copy-start.6
  484.5 4.0 copy-start.2
  493.3 316.8 %all-gather.10.cloned.1.call-start = ((), (), s32[]{:S(2)}) async-start(), calls=%async_computation.5 | async-start | bytes 18874368 | tf_op jit(solution)/shard_map/all_gather | solution.py:12
  611.0 7.8 copy-start.3
  611.0 7.8 copy-start.13
  624.5 337.3 %all-reduce.8.cloned.1.call-start = ((), (), s32[]{:S(2)}) async-start(), calls=%async_computation.3 | async-start | bytes 1048576 | tf_op jit(solution)/shard_map/psum | solution.py:82
  833.4 2.2 copy-start.4
  835.6 3.9 copy-start.7
Sparse Core Ops, SparseCore 0:
  9.6 37.4 all-gather.5
  143.1 118.4 all-reduce.3
  275.4 185.3 all-gather.7
  493.5 117.4 all-reduce.5
  624.6 185.4 all-gather.9
  844.3 117.4 all-reduce.7
